TPU v7x, 512 devices: a whole 4x8x8 slice. The times are simulated.
512 devices in a mesh: energy: 64 (over x, y, core), cuts: 8 (over z).
Axes of the slice: x: 4, y: 8, z: 8, core: 2. Of those that a mesh axis runs over, the one named last changes fastest.
Arguments:
- g_lesser: float32 [2, 512, 8, 4096], P(None, 'energy', 'cuts'), may hold values from -6 to 6
- g_greater: float32 [2, 512, 8, 4096], P(None, 'energy', 'cuts'), may hold values from -6 to 6
- v_blocks: float32 [8, 64, 64], P('cuts'), may hold values from -0.75 to 0.75
- slots: int32 [8, 4096], P('cuts'), may hold values from 0 to 8191
Outputs:
- screened: float32 [2, 512, 8, 4096], P(None, 'energy', 'cuts')
Inputs may be any that keep to these rules, and one draw needn't show every extreme that they name: slots[s, k] = row * 2 * 64 + column of element k of slice s, rows of the slice's orbitals, columns below 64 in the slice's own block and the others in its block towards the next slice; positions may repeat and then add.
All inputs are finite; a program needn't handle non-finite values.
Results may differ from a plain program's by a relative error of at most 0.0001.
Values sent between devices are 32-bit elements; how exact they have to be, the bound alone decides.
No kernel may reach another device: no remote copies, remote signals or barrier semaphores. Data moves between devices by JAX's collectives and lax.ppermute only.
A program may use at most 64 MiB of HBM per device.

v0:
```python
import functools
import math

import jax
import jax.numpy as jnp
import numpy as np
from jax import lax
from jax.experimental import pallas as pl
from jax.experimental.pallas import tpu as pltpu
from jax.sharding import PartitionSpec as P

SCREEN = 0.08
F32 = jnp.float32
BF16 = jnp.bfloat16
LANES = 128
HALF = 64


def split(x):
    high = x.astype(BF16)
    return high, (x - high.astype(F32)).astype(BF16)


def left_half(shape):
    return lax.broadcasted_iota(jnp.int32, shape, len(shape) - 1) < HALF


def dot(a, b):
    return jnp.dot(a, b, preferred_element_type=F32)


def pack_kernel(lesser_ref, greater_ref, out_ref):
    left = left_half((8, LANES))
    for tile in range(32):
        for which, ref in enumerate((lesser_ref, greater_ref)):
            real = ref[pl.ds(tile, 8, stride=32), :]
            imag = ref[pl.ds(256 + tile, 8, stride=32), :]
            rows = pl.ds(which * 8, 8)
            out_ref[2 * tile, rows, :] = jnp.where(left, real, pltpu.roll(imag, HALF, 1))
            out_ref[2 * tile + 1, rows, :] = jnp.where(left, pltpu.roll(real, HALF, 1), imag)


def correlate_kernel(data_ref, high_ref, low_ref, turn_ref, out_ref):
    count = 512
    lesser = data_ref[:, 0].reshape(count, LANES)
    greater = data_ref[:, 1].reshape(count, LANES)
    left = left_half((count, LANES))
    sign = jnp.where(left, 1.0, -1.0).astype(F32)

    def turned(x):
        return pltpu.roll(x, HALF, 1)

    signals = jnp.concatenate([lesser, greater], axis=1)
    sig_high, sig_low = split(signals)

    def transform(rows):
        table_high, table_low = high_ref[rows, :], low_ref[rows, :]
        return (
            dot(table_high, sig_high) + dot(table_high, sig_low) + dot(table_low, sig_high)
        )

    cosines = transform(pl.ds(0, count))
    sines = transform(pl.ds(count, count))
    cos_a, cos_b = cosines[:, :LANES], cosines[:, LANES:]
    sin_a, sin_b = sines[:, :LANES], sines[:, LANES:]
    shift_a, shift_b = sign * turned(sin_a), sign * turned(sin_b)

    def times_conjugate(a, b):
        other_b = turned(b)
        real_b = jnp.where(left, b, other_b)
        imag_b = jnp.where(left, other_b, b)
        return a * real_b + (sign * turned(a)) * imag_b

    plus = times_conjugate(cos_a + shift_a, cos_b + shift_b)
    minus = times_conjugate(cos_a - shift_a, cos_b - shift_b)
    for_cos = -sign * turned(plus + minus)
    for_sin = minus - plus
    turn_cos, turn_sin = turn_ref[0], turn_ref[1]
    cos_high, cos_low = split(turn_cos * for_cos - turn_sin * for_sin)
    sin_high, sin_low = split(turn_sin * for_cos + turn_cos * for_sin)
    cos_rows, sin_rows = pl.ds(0, count), pl.ds(count, count)
    result = dot(high_ref[cos_rows, :], cos_high) + dot(high_ref[sin_rows, :], sin_high)
    result += dot(high_ref[cos_rows, :], cos_low) + dot(high_ref[sin_rows, :], sin_low)
    result += dot(low_ref[cos_rows, :], cos_high) + dot(low_ref[sin_rows, :], sin_high)
    out_ref[...] = result


def repeated_row(ref, row):
    return jnp.broadcast_to(ref[pl.ds(row, 1), :], (16, LANES)).astype(BF16)


def screen_kernel(polar_ref, side_ref, out_ref, parts_ref, first_ref, second_ref, lines_ref, y_ref):
    left32 = left_half((32, LANES))
    row_iota = lax.broadcasted_iota(jnp.int32, (32, LANES), 0).astype(F32).astype(BF16)
    column_iota = lax.broadcasted_iota(jnp.int32, (256, LANES), 0).astype(F32).astype(BF16)
    zero = jnp.zeros((), BF16)
    one = jnp.ones((), BF16)

    def join(even, odd):
        return jnp.where(left32, even, pltpu.roll(odd, HALF, 1))

    def join_right(even, odd):
        return jnp.where(left32, pltpu.roll(even, HALF, 1), odd)

    def one_slice(s, carry):
        even = polar_ref[pl.ds(s, 32, stride=16), :]
        odd = polar_ref[pl.ds(s + 8, 32, stride=16), :]
        real_high, real_low = split(join(even, odd))
        imag_high, imag_low = split(join_right(even, odd))
        for i, part in enumerate((real_high, real_low, imag_high, imag_low)):
            parts_ref[i] = part.astype(F32)
        side = side_ref.at[s]
        slot = join_right(side[pl.ds(0, 32, stride=2), :], side[pl.ds(1, 32, stride=2), :])
        slot = slot.astype(jnp.int32)
        column = slot & 127
        moved = HALF + (column & 1) * 32 + ((column - HALF) >> 1)
        column = jnp.where(column < HALF, column, moved)
        lines_ref[0] = (slot >> 8).astype(F32)
        lines_ref[1] = ((slot & 128) + column).astype(F32)

        for r in range(32):
            lane = pl.ds(r * LANES, LANES)
            hit = jnp.concatenate([repeated_row(lines_ref.at[0], r)] * 2, axis=0) == row_iota
            for i in range(4):
                value = jnp.concatenate([repeated_row(parts_ref.at[i], r)] * 2, axis=0)
                first_ref[pl.ds(i * 32, 32), lane] = jnp.where(hit, value, zero)
            place = jnp.concatenate([repeated_row(lines_ref.at[1], r)] * 16, axis=0) == column_iota
            second_ref[:, lane] = jnp.where(place, one, zero)
        dense = lax.dot_general(
            first_ref[...], second_ref[...], (((1,), (1,)), ((), ())), preferred_element_type=F32
        )
        real = dense[0:32] + dense[32:64]
        imag = dense[64:96] + dense[96:128]
        dense = jnp.concatenate(
            [
                jnp.concatenate([real[:, :LANES], imag[:, :LANES]], axis=1),
                jnp.concatenate([real[:, LANES:], imag[:, LANES:]], axis=1),
            ],
            axis=0,
        )
        dense_high, dense_low = split(dense)
        v_high, v_low = split(side_ref[s][:, :HALF])
        y_ref[s] = dot(v_high, dense_high) + dot(v_high, dense_low) + dot(v_low, dense_high)
        return carry

    lax.fori_loop(0, 8, one_slice, 0)

    real = y_ref[0][:, :HALF]
    imag = y_ref[0][:, LANES : LANES + HALF]
    for s in range(8):
        y = y_ref[s]
        if s:
            couple_real = SCREEN * y[:, HALF:LANES]
            couple_imag = SCREEN * y[:, LANES + HALF :]
            matrix = jnp.concatenate(
                [
                    jnp.concatenate([couple_real, -couple_imag], axis=1),
                    jnp.concatenate([couple_imag, couple_real], axis=1),
                ],
                axis=0,
            )
            m_high, m_low = split(matrix)
            x_high, x_low = split(jnp.concatenate([real, imag], axis=0))
            product = dot(m_high, x_high) + dot(m_high, x_low) + dot(m_low, x_high)
            real = product[:HALF] + y[:, :HALF]
            imag = product[HALF:] + y[:, LANES : LANES + HALF]
        out_ref[s, 0] = jnp.concatenate([real[:32], real[32:]], axis=1)
        out_ref[s, 1] = jnp.concatenate([imag[:32], imag[32:]], axis=1)


def tables(count):
    half = np.arange(count) + 0.5
    angle = np.outer(half, half) * (math.pi / count)
    table = np.concatenate([np.cos(angle), np.sin(angle)]).astype(np.float32)
    high = table.astype(jnp.bfloat16)
    low = (table - high.astype(np.float32)).astype(jnp.bfloat16)
    turn = half * (math.pi / count) / 2
    scale = 1.0 / (2 * count * math.sqrt(count))
    turns = np.stack([np.cos(turn), np.sin(turn)]) * scale
    turns = np.broadcast_to(turns[:, :, None], (2, count, LANES)).astype(np.float32)
    return high, low, np.ascontiguousarray(turns)


def vmem(n):
    return [pl.BlockSpec(memory_space=pltpu.VMEM)] * n


def pack(lesser, greater):
    return pl.pallas_call(
        pack_kernel,
        out_shape=jax.ShapeDtypeStruct((64, 16, LANES), F32),
        in_specs=vmem(2),
        out_specs=vmem(1)[0],
        name="pack",
    )(lesser.reshape(512, LANES), greater.reshape(512, LANES))


def correlate(data):
    high, low, turns = tables(512)
    return pl.pallas_call(
        correlate_kernel,
        out_shape=jax.ShapeDtypeStruct((512, LANES), F32),
        in_specs=vmem(4),
        out_specs=vmem(1)[0],
        compiler_params=pltpu.CompilerParams(vmem_limit_bytes=40 << 20),
        name="correlate",
    )(data.reshape(64, 2, 8, LANES), jnp.asarray(high), jnp.asarray(low), jnp.asarray(turns))


def screen(polar, side):
    return pl.pallas_call(
        screen_kernel,
        out_shape=jax.ShapeDtypeStruct((8, 2, 32, LANES), F32),
        in_specs=vmem(2),
        out_specs=vmem(1)[0],
        scratch_shapes=[
            pltpu.VMEM((4, 32, LANES), F32),
            pltpu.VMEM((LANES, 4096), BF16),
            pltpu.VMEM((256, 4096), BF16),
            pltpu.VMEM((2, 32, LANES), F32),
            pltpu.VMEM((8, HALF, 256), F32),
        ],
        compiler_params=pltpu.CompilerParams(vmem_limit_bytes=40 << 20),
        name="screen",
    )(polar, side)


def side_rows(v_blocks, slots):
    v = v_blocks.reshape(32, 2, 32, 2).transpose(1, 0, 3, 2).reshape(HALF, HALF)
    return jnp.concatenate([v, slots.reshape(HALF, HALF).astype(F32)], axis=1)


def shards(g_lesser, g_greater, v_blocks, slots):
    side = lax.all_gather(side_rows(v_blocks, slots), "cuts")
    data = lax.all_to_all(pack(g_lesser, g_greater), "energy", 0, 0, tiled=True)
    polar = correlate(data)
    polar = lax.all_to_all(
        polar.reshape(512, 1, LANES), ("energy", "cuts"), 0, 0, tiled=True
    ).reshape(512, LANES)
    blocks = screen(polar, side).reshape(8, 64, LANES)
    blocks = lax.all_to_all(blocks, "cuts", 0, 0, tiled=True)
    return blocks.reshape(8, 2, 4096).transpose(1, 0, 2).reshape(2, 8, 1, 4096)


def solution(mesh):
    placed = (
        P(None, "energy", "cuts", None),
        P(None, "energy", "cuts", None),
        P("cuts", None, None),
        P("cuts", None),
    )
    return jax.shard_map(
        shards,
        mesh=mesh,
        in_specs=placed,
        out_specs=P(None, "energy", "cuts", None),
        check_vma=False,
    )
```

profile of v0, /device:TPU:2, one launch (start us, length us, event | category | flops | bytes accessed | tf_op | source)
XLA Modules:
  0.0 111.4 jit_solution(3701455868350236659)
XLA Ops:
  0.0 0.0 copy-start
  0.0 0.0 copy-start.1
  0.0 2.4 %pack.1 = f32[64,16,128]{2,1,0:T(8,128)} custom-call(f32[512,128]{1,0:T(8,128)} %bitcast.19, f32[512,128]{1,0:T(8,128)} %bitcast.20), custom_call_target="tpu_custom_call" | custom-call | tf_op jit(solution)/shard_map/pack/pallas_call | solution.py:189
  2.4 27.3 %all_to_all.15 = f32[64,16,128]{2,1,0:T(8,128)S(1)} all-to-all(f32[64,16,128]{2,1,0:T(8,128)} %pack.1), channel_id=1, replica_groups=mesh['energy'=64,'cuts'=8] {'energy'}, dimensions={0} | all-to-all | bytes 1048576 | tf_op jit(solution)/shard_map/all_to_all | solution.py:235
  29.7 0.0 copy-done
  29.7 0.0 copy-done.1
  29.7 0.0 copy-start.2
  29.7 1.0 copy-done.2
  30.8 4.5 %correlate.1 = f32[512,128]{1,0:T(8,128)} custom-call(f32[64,2,8,128]{3,2,1,0:T(8,128)S(1)} %bitcast.13, bf16[1024,512]{1,0:T(8,128)(2,1)S(1)} %copy-done, bf16[1024,512]{1,0:T(8,128)(2,1)S(1)} %copy-done.1, f32[2,512,128]{2,1,0:T(8,128)S(1)} %copy-done.2), custom_call_target="tpu_custom_call" | custom-call | tf_op jit(solution)/shard_map/correlate/pallas_call | solution.py:200
  35.3 0.0 copy-start.3
  35.3 17.4 %all-to-all-start.1 = ((f32[512,1,128]{2,1,0:T(1,128)}), f32[512,1,128]{2,1,0:T(1,128)S(1)}, u32[]{:S(2)}, u32[]{:S(2)}) async-start(f32[512,1,128]{2,1,0:T(1,128)} %bitcast.4), calls=%async_computation.1 | async-start | bytes 524288 | tf_op jit(solution)/shard_map/all_to_all | solution.py:237
  52.8 0.0 copy-done.3
  52.8 1.1 reshape.37
  53.8 0.5 copy.13
  54.3 0.0 copy-start.4
  54.3 0.1 reshape.38
  54.4 0.6 copy-done.4
  55.1 0.1 convert_element_type.7
  55.2 0.1 pad_maximum_fusion
  55.2 28.9 %all-gather = f32[512,128]{1,0:T(8,128)S(1)} all-gather(f32[64,128]{1,0:T(8,128)S(1)} %pad_maximum_fusion), channel_id=2, replica_groups=mesh['energy'=64,'cuts'=8] {'cuts'}, dimensions={0}, use_global_device_ids=true | all-gather | bytes 294912 | tf_op jit(solution)/shard_map/all_gather | solution.py:234
  84.2 0.0 all-to-all-done.1
  84.2 11.2 %screen.1 = f32[8,2,32,128]{3,2,1,0:T(8,128)S(1)} custom-call(f32[512,128]{1,0:T(8,128)S(1)} %bitcast.14, f32[8,64,128]{2,1,0:T(8,128)S(1)} %bitcast.15), custom_call_target="tpu_custom_call" | custom-call | tf_op jit(solution)/shard_map/screen/pallas_call | solution.py:211
  95.4 14.9 %all_to_all.16 = f32[8,64,128]{2,1,0:T(8,128)S(1)} all-to-all(f32[8,64,128]{2,1,0:T(8,128)S(1)} %bitcast.16), channel_id=1, replica_groups=mesh['energy'=64,'cuts'=8] {'cuts'}, dimensions={0} | all-to-all | bytes 524288 | tf_op jit(solution)/shard_map/all_to_all | solution.py:241
  110.3 0.1 reshape.40
  110.4 1.0 copy.14
  (1 shorter events, 0.0 us)
Async XLA Ops:
  0.0 29.7 %copy-start = (bf16[1024,512]{1,0:T(8,128)(2,1)S(1)}, bf16[1024,512]{1,0:T(8,128)(2,1)}, u32[]{:S(2)}) copy-start(bf16[1024,512]{1,0:T(8,128)(2,1)} %constant.6.clone.high_ref) | copy-start | bytes 3145732
  0.0 29.7 %copy-start.1 = (bf16[1024,512]{1,0:T(8,128)(2,1)S(1)}, bf16[1024,512]{1,0:T(8,128)(2,1)}, u32[]{:S(2)}) copy-start(bf16[1024,512]{1,0:T(8,128)(2,1)} %constant.7.clone.low_ref) | copy-start | bytes 3145732
  29.7 1.0 copy-start.2
  35.3 17.5 %copy-start.3 = (f32[1,64,64]{2,1,0:T(8,128)S(1)}, f32[1,64,64]{2,1,0:T(8,128)}, u32[]{:S(2)}) copy-start(f32[1,64,64]{2,1,0:T(8,128)} %param.9) | copy-start | bytes 49156
  35.3 48.9 %all-to-all-start.1 = ((f32[512,1,128]{2,1,0:T(1,128)}), f32[512,1,128]{2,1,0:T(1,128)S(1)}, u32[]{:S(2)}, u32[]{:S(2)}) async-start(f32[512,1,128]{2,1,0:T(1,128)} %bitcast.4), calls=%async_computation.1 | async-start | bytes 524288 | tf_op jit(solution)/shard_map/all_to_all | solution.py:237
  54.3 0.7 copy-start.4
where the time goes:
time: 112 us; the launch traced here: 111 us
  blocking collectives  71.2 us (64%)
  Pallas kernels  18.1 us (16%)
  starting transfers between devices  17.4 us (16%)
  local copies, waits for them, and re-layouts  4.49 us (4%)
    all_gather x1, blocking collectives, shards(): side = lax.all_gather(side_rows(v_blocks, slots), 'cuts')  28.9 us
    all_to_all x1, blocking collectives, shards(): data = lax.all_to_all(pack(g_lesser, g_greater), 'energy', 0, 0, tiled=True)  27.3 us
    all_to_all x1, starting transfers between devices, shards(): lax.all_to_all(polar.reshape(512, 1, LANES), ('energy', 'cuts'), 0, 0, ti...  17.4 us
    all_to_all x1, blocking collectives, shards(): blocks = lax.all_to_all(blocks, 'cuts', 0, 0, tiled=True)  14.9 us
    pallas_call x1, Pallas kernels, screen(): pl.pallas_call(screen_kernel, out_shape=jax.ShapeDtypeStruct((8, 2, 32, L...  11.2 us
    pallas_call x1, Pallas kernels, correlate(): pl.pallas_call(correlate_kernel, out_shape=jax.ShapeDtypeStruct((512, LAN...  4.54 us
    pallas_call x1, Pallas kernels, pack(): pl.pallas_call(pack_kernel, out_shape=jax.ShapeDtypeStruct((64, 16, LANES...  2.36 us
  transfers between devices with their start and end apart: 1, of which 0 were waited for; matrix products, arithmetic and copies ran while one was open for 2% of the time, Pallas kernels for 0%

commit v1 on v0

--- a/solution.py
+++ b/solution.py
@@ -14,6 +14,7 @@
 BF16 = jnp.bfloat16
 LANES = 128
 HALF = 64
+SIDE = 256
 
 
 def split(x):
@@ -29,7 +30,10 @@
     return jnp.dot(a, b, preferred_element_type=F32)
 
 
-def pack_kernel(lesser_ref, greater_ref, out_ref):
+def pack_kernel(lesser_ref, greater_ref, v_ref, slots_ref, out_ref, side_ref):
+    side_ref[pl.ds(0, 32), :] = slots_ref[...].astype(F32)
+    side_ref[pl.ds(32, HALF), :] = jnp.concatenate([v_ref[0], v_ref[0]], axis=1)
+    side_ref[pl.ds(96, SIDE - 96), :] = jnp.zeros((SIDE - 96, LANES), F32)
     left = left_half((8, LANES))
     for tile in range(32):
         for which, ref in enumerate((lesser_ref, greater_ref)):
@@ -40,8 +44,9 @@
             out_ref[2 * tile + 1, rows, :] = jnp.where(left, pltpu.roll(real, HALF, 1), imag)
 
 
-def correlate_kernel(data_ref, high_ref, low_ref, turn_ref, out_ref):
+def correlate_kernel(data_ref, table_ref, out_ref):
     count = 512
+    high_ref, low_ref = table_ref.at[pl.ds(0, 2 * count)], table_ref.at[pl.ds(2 * count, 2 * count)]
     lesser = data_ref[:, 0].reshape(count, LANES)
     greater = data_ref[:, 1].reshape(count, LANES)
     left = left_half((count, LANES))
@@ -75,7 +80,13 @@
     minus = times_conjugate(cos_a - shift_a, cos_b - shift_b)
     for_cos = -sign * turned(plus + minus)
     for_sin = minus - plus
-    turn_cos, turn_sin = turn_ref[0], turn_ref[1]
+    scale = 1.0 / (2 * count * math.sqrt(count))
+
+    def turn(rows):
+        column = high_ref[rows, :LANES][:, :1].astype(F32) + low_ref[rows, :LANES][:, :1].astype(F32)
+        return jnp.broadcast_to(column * scale, (count, LANES))
+
+    turn_cos, turn_sin = turn(pl.ds(0, count)), turn(pl.ds(count, count))
     cos_high, cos_low = split(turn_cos * for_cos - turn_sin * for_sin)
     sin_high, sin_low = split(turn_sin * for_cos + turn_cos * for_sin)
     cos_rows, sin_rows = pl.ds(0, count), pl.ds(count, count)
@@ -110,13 +121,12 @@
         for i, part in enumerate((real_high, real_low, imag_high, imag_low)):
             parts_ref[i] = part.astype(F32)
         side = side_ref.at[s]
-        slot = join_right(side[pl.ds(0, 32, stride=2), :], side[pl.ds(1, 32, stride=2), :])
-        slot = slot.astype(jnp.int32)
+        slot = side[pl.ds(0, 32), :].astype(jnp.int32)
         column = slot & 127
         moved = HALF + (column & 1) * 32 + ((column - HALF) >> 1)
         column = jnp.where(column < HALF, column, moved)
-        lines_ref[0] = (slot >> 8).astype(F32)
-        lines_ref[1] = ((slot & 128) + column).astype(F32)
+        lines_ref[0] = ((slot >> 7) & 31).astype(F32)
+        lines_ref[1] = (((slot >> 12) << 7) + column).astype(F32)
 
         for r in range(32):
             lane = pl.ds(r * LANES, LANES)
@@ -139,7 +149,8 @@
             axis=0,
         )
         dense_high, dense_low = split(dense)
-        v_high, v_low = split(side_ref[s][:, :HALF])
+        rows = [side[pl.ds(32 + parity, 32, stride=2), :] for parity in range(2)]
+        v_high, v_low = split(jnp.concatenate(rows, axis=0)[:, :HALF])
         y_ref[s] = dot(v_high, dense_high) + dot(v_high, dense_low) + dot(v_low, dense_high)
         return carry
 
@@ -174,37 +185,40 @@
     table = np.concatenate([np.cos(angle), np.sin(angle)]).astype(np.float32)
     high = table.astype(jnp.bfloat16)
     low = (table - high.astype(np.float32)).astype(jnp.bfloat16)
-    turn = half * (math.pi / count) / 2
-    scale = 1.0 / (2 * count * math.sqrt(count))
-    turns = np.stack([np.cos(turn), np.sin(turn)]) * scale
-    turns = np.broadcast_to(turns[:, :, None], (2, count, LANES)).astype(np.float32)
-    return high, low, np.ascontiguousarray(turns)
+    return np.concatenate([high, low])
 
 
 def vmem(n):
     return [pl.BlockSpec(memory_space=pltpu.VMEM)] * n
 
 
-def pack(lesser, greater):
+def pack(lesser, greater, v_blocks, slots):
     return pl.pallas_call(
         pack_kernel,
-        out_shape=jax.ShapeDtypeStruct((64, 16, LANES), F32),
-        in_specs=vmem(2),
-        out_specs=vmem(1)[0],
+        out_shape=(
+            jax.ShapeDtypeStruct((64, 16, LANES), F32),
+            jax.ShapeDtypeStruct((SIDE, LANES), F32),
+        ),
+        in_specs=vmem(4),
+        out_specs=tuple(vmem(2)),
         name="pack",
-    )(lesser.reshape(512, LANES), greater.reshape(512, LANES))
+    )(
+        lesser.reshape(512, LANES),
+        greater.reshape(512, LANES),
+        v_blocks,
+        slots.reshape(32, LANES),
+    )
 
 
 def correlate(data):
-    high, low, turns = tables(512)
     return pl.pallas_call(
         correlate_kernel,
         out_shape=jax.ShapeDtypeStruct((512, LANES), F32),
-        in_specs=vmem(4),
+        in_specs=vmem(2),
         out_specs=vmem(1)[0],
         compiler_params=pltpu.CompilerParams(vmem_limit_bytes=40 << 20),
         name="correlate",
-    )(data.reshape(64, 2, 8, LANES), jnp.asarray(high), jnp.asarray(low), jnp.asarray(turns))
+    )(data.reshape(64, 2, 8, LANES), jnp.asarray(tables(512)))
 
 
 def screen(polar, side):
@@ -225,14 +239,10 @@
     )(polar, side)
 
 
-def side_rows(v_blocks, slots):
-    v = v_blocks.reshape(32, 2, 32, 2).transpose(1, 0, 3, 2).reshape(HALF, HALF)
-    return jnp.concatenate([v, slots.reshape(HALF, HALF).astype(F32)], axis=1)
-
-
 def shards(g_lesser, g_greater, v_blocks, slots):
-    side = lax.all_gather(side_rows(v_blocks, slots), "cuts")
-    data = lax.all_to_all(pack(g_lesser, g_greater), "energy", 0, 0, tiled=True)
+    data, side = pack(g_lesser, g_greater, v_blocks, slots)
+    side = lax.all_gather(side, "cuts")
+    data = lax.all_to_all(data, "energy", 0, 0, tiled=True)
     polar = correlate(data)
     polar = lax.all_to_all(
         polar.reshape(512, 1, LANES), ("energy", "cuts"), 0, 0, tiled=True

time: 112 us -> 111 us (level)
  the two profiles are of different devices: /device:TPU:2 before, /device:TPU:9 now
where the time goes in v1:
time: 111 us; the launch traced here: 110 us
  blocking collectives  76.2 us (69%)
  Pallas kernels  16.9 us (15%)
  between operations  13.4 us (12%)
  local copies, waits for them, and re-layouts  3.94 us (4%)
    all_to_all x1, blocking collectives, shards(): lax.all_to_all(polar.reshape(512, 1, LANES), ('energy', 'cuts'), 0, 0, ti...  33 us
    all_to_all x1, blocking collectives, shards(): data = lax.all_to_all(data, 'energy', 0, 0, tiled=True)  27.7 us
    all_to_all x1, blocking collectives, shards(): blocks = lax.all_to_all(blocks, 'cuts', 0, 0, tiled=True)  15.5 us
    pallas_call x1, Pallas kernels, screen(): pl.pallas_call(screen_kernel, out_shape=jax.ShapeDtypeStruct((8, 2, 32, L...  10.8 us
    pallas_call x1, Pallas kernels, correlate(): pl.pallas_call(correlate_kernel, out_shape=jax.ShapeDtypeStruct((512, LAN...  3.85 us
    unnamed x4, local copies, waits for them, and re-layouts  2.83 us
    pallas_call x1, Pallas kernels, pack(): pl.pallas_call(pack_kernel, out_shape=(jax.ShapeDtypeStruct((64, 16, LANE...  2.23 us
  transfers between devices with their start and end apart: 1, of which 0 were waited for; matrix products, arithmetic and copies ran while one was open for 0% of the time, Pallas kernels for 3%

profile of v1, /device:TPU:9, one launch (start us, length us, event | category | flops | bytes accessed | tf_op | source)
XLA Modules:
  0.0 110.4 jit_solution(14109033187135941715)
XLA Ops:
  6.5 0.0 all-gather.3.cloned.1.call-start
  6.5 2.2 %pack.1 = (f32[64,16,128]{2,1,0:T(8,128)}, f32[256,128]{1,0:T(8,128)}) custom-call(f32[512,128]{1,0:T(8,128)} %bitcast.19, f32[512,128]{1,0:T(8,128)} %bitcast.20, f32[1,64,64]{2,1,0:T(8,128)} %v_ref.1, s32[32,128]{1,0:T(8,128)} %bitcast.21), custom_call_target="tpu_custom_call" | custom-call | tf_op jit(solution)/shard_map/pack/pallas_call | solution.py:196
  8.8 0.0 all-gather.3.cloned.1.call-update
  8.8 27.7 %all_to_all.15 = f32[64,16,128]{2,1,0:T(8,128)S(1)} all-to-all(f32[64,16,128]{2,1,0:T(8,128)} %get-tuple-element.7), channel_id=1, replica_groups=mesh['energy'=64,'cuts'=8] {'energy'}, dimensions={0} | all-to-all | bytes 1048576 | tf_op jit(solution)/shard_map/all_to_all | solution.py:245
  36.5 0.0 copy-start
  36.5 1.6 %copy-done = bf16[2048,512]{1,0:T(8,128)(2,1)S(1)} copy-done((bf16[2048,512]{1,0:T(8,128)(2,1)S(1)}, bf16[2048,512]{1,0:T(8,128)(2,1)}, u32[]{:S(2)}) %copy-start) | copy-done | bytes 2097176
  38.1 3.9 %correlate.1 = f32[512,128]{1,0:T(8,128)S(1)} custom-call(f32[64,2,8,128]{3,2,1,0:T(8,128)S(1)} %bitcast.13, bf16[2048,512]{1,0:T(8,128)(2,1)S(1)} %copy-done), custom_call_target="tpu_custom_call" | custom-call | tf_op jit(solution)/shard_map/correlate/pallas_call | solution.py:214
  42.0 33.0 %all_to_all.16 = f32[512,1,128]{2,1,0:T(1,128)S(1)} all-to-all(f32[512,1,128]{2,1,0:T(1,128)S(1)} %bitcast.17), channel_id=1, replica_groups=mesh['energy'=64,'cuts'=8] {'energy','cuts'}, dimensions={0} | all-to-all | bytes 524288 | tf_op jit(solution)/shard_map/all_to_all | solution.py:247
  74.9 0.0 all-gather.3.cloned.1.call-done
  74.9 0.0 copy-start.1
  74.9 1.2 %copy-done.1 = f32[2048,128]{1,0:T(8,128)S(1)} copy-done((f32[2048,128]{1,0:T(8,128)S(1)}, f32[2048,128]{1,0:T(8,128)}, u32[]{:S(2)}) %copy-start.1) | copy-done | bytes 1048600
  76.2 10.8 %screen.1 = f32[8,2,32,128]{3,2,1,0:T(8,128)S(1)} custom-call(f32[512,128]{1,0:T(8,128)S(1)} %bitcast.15, f32[8,256,128]{2,1,0:T(8,128)S(1)} %bitcast.14), custom_call_target="tpu_custom_call" | custom-call | tf_op jit(solution)/shard_map/screen/pallas_call | solution.py:225
  87.0 15.5 %all_to_all.17 = f32[8,64,128]{2,1,0:T(8,128)S(1)} all-to-all(f32[8,64,128]{2,1,0:T(8,128)S(1)} %bitcast.16), channel_id=1, replica_groups=mesh['energy'=64,'cuts'=8] {'cuts'}, dimensions={0} | all-to-all | bytes 524288 | tf_op jit(solution)/shard_map/all_to_all | solution.py:251
  102.5 0.1 reshape.34
  102.6 1.0 copy.8
Async XLA Ops:
  6.5 68.4 %all-gather.3.cloned.1.call-start = ((), (), s32[]{:S(2)}) async-start(), calls=%async_computation.3 | async-start | bytes 1179648 | tf_op jit(solution)/shard_map/all_gather | solution.py:244
  36.5 1.6 %copy-start = (bf16[2048,512]{1,0:T(8,128)(2,1)S(1)}, bf16[2048,512]{1,0:T(8,128)(2,1)}, u32[]{:S(2)}) copy-start(bf16[2048,512]{1,0:T(8,128)(2,1)} %constant.2.clone.table_ref) | copy-start | bytes 6291460
  74.9 1.2 %copy-start.1 = (f32[2048,128]{1,0:T(8,128)S(1)}, f32[2048,128]{1,0:T(8,128)}, u32[]{:S(2)}) copy-start(f32[2048,128]{1,0:T(8,128)} %all-gather.3.cloned.1.call-done) | copy-start | bytes 3145732
Sparse Core Ops, SparseCore 0:
  9.4 42.2 all-gather.2

commit v2 on v0

v2 whole, which is shorter than its diff:
```python
import functools
import math

import jax
import jax.numpy as jnp
import numpy as np
from jax import lax
from jax.experimental import pallas as pl
from jax.experimental.pallas import tpu as pltpu
from jax.sharding import PartitionSpec as P

SCREEN = 0.08
F32 = jnp.float32
BF16 = jnp.bfloat16
LANES = 128
HALF = 64


def split(x):
    high = x.astype(BF16)
    return high, (x - high.astype(F32)).astype(BF16)


def left_half(shape):
    return lax.broadcasted_iota(jnp.int32, shape, len(shape) - 1) < HALF


def dot(a, b):
    return jnp.dot(a, b, preferred_element_type=F32)


def pack_kernel(lesser_ref, greater_ref, out_ref):
    left = left_half((8, LANES))
    for tile in range(32):
        for which, ref in enumerate((lesser_ref, greater_ref)):
            real = ref[pl.ds(tile, 8, stride=32), :]
            imag = ref[pl.ds(256 + tile, 8, stride=32), :]
            rows = pl.ds(which * 8, 8)
            out_ref[2 * tile, rows, :] = jnp.where(left, real, pltpu.roll(imag, HALF, 1))
            out_ref[2 * tile + 1, rows, :] = jnp.where(left, pltpu.roll(real, HALF, 1), imag)


def correlate_kernel(data_ref, v_ref, slots_ref, table_hbm, out_ref, table_ref, sems):
    count = 512
    copies = []
    for i in range(4):
        rows = pl.ds(i * count, count)
        copies.append(pltpu.make_async_copy(table_hbm.at[rows], table_ref.at[i], sems.at[i]))
        copies[i].start()
    left = left_half((count, LANES))
    sign = jnp.where(left, 1.0, -1.0).astype(F32)

    def turned(x):
        return pltpu.roll(x, HALF, 1)

    me = lax.axis_index("energy")
    slot = slots_ref[pl.ds(me // 2, 1), :].astype(F32)
    slot = jnp.where(me % 2 == 0, slot, turned(slot))[:, :HALF]
    side = jnp.concatenate([slot, v_ref[0, pl.ds(me, 1), :]], axis=1)
    out_ref[pl.ds(1, count, stride=2), :] = jnp.broadcast_to(side, (count, LANES))

    lesser = data_ref[:, 0].reshape(count, LANES)
    greater = data_ref[:, 1].reshape(count, LANES)
    sig_high, sig_low = split(jnp.concatenate([lesser, greater], axis=1))
    both = jnp.concatenate([sig_high, sig_low], axis=1)
    copies[0].wait()
    cosines = dot(table_ref[0], both)
    copies[1].wait()
    sines = dot(table_ref[1], both)
    copies[2].wait()
    cosines = cosines[:, :256] + cosines[:, 256:] + dot(table_ref[2], sig_high)
    copies[3].wait()
    sines = sines[:, :256] + sines[:, 256:] + dot(table_ref[3], sig_high)
    cos_a, cos_b = cosines[:, :LANES], cosines[:, LANES:]
    sin_a, sin_b = sines[:, :LANES], sines[:, LANES:]
    shift_a, shift_b = sign * turned(sin_a), sign * turned(sin_b)

    def times_conjugate(a, b):
        other_b = turned(b)
        real_b = jnp.where(left, b, other_b)
        imag_b = jnp.where(left, other_b, b)
        return a * real_b + (sign * turned(a)) * imag_b

    plus = times_conjugate(cos_a + shift_a, cos_b + shift_b)
    minus = times_conjugate(cos_a - shift_a, cos_b - shift_b)
    for_cos = -sign * turned(plus + minus)
    for_sin = minus - plus
    scale = 1.0 / (2 * count * math.sqrt(count))

    def turn(i):
        column = table_ref[i, :, :LANES][:, :1].astype(F32)
        column += table_ref[i + 2, :, :LANES][:, :1].astype(F32)
        return jnp.broadcast_to(column * scale, (count, LANES))

    turn_cos, turn_sin = turn(0), turn(1)
    cos_high, cos_low = split(turn_cos * for_cos - turn_sin * for_sin)
    sin_high, sin_low = split(turn_sin * for_cos + turn_cos * for_sin)
    result = dot(table_ref[0], jnp.concatenate([cos_high, cos_low], axis=1))
    result += dot(table_ref[1], jnp.concatenate([sin_high, sin_low], axis=1))
    result = result[:, :LANES] + result[:, LANES:]
    result += dot(table_ref[2], cos_high) + dot(table_ref[3], sin_high)
    out_ref[pl.ds(0, count, stride=2), :] = result


def repeated_row(ref, row, times):
    tile = jnp.broadcast_to(ref[pl.ds(row, 1), :], (16, LANES)).astype(BF16)
    return jnp.concatenate([tile] * times, axis=0)


def screen_kernel(data_ref, out_ref, parts_ref, lines_ref, dense_ref):
    left32 = left_half((32, LANES))
    row_iota = lax.broadcasted_iota(jnp.int32, (HALF, LANES), 0).astype(F32).astype(BF16)
    column_iota = lax.broadcasted_iota(jnp.int32, (LANES, LANES), 0).astype(F32).astype(BF16)
    zero = jnp.zeros((), BF16)
    one = jnp.ones((), BF16)

    def lines(s, side):
        return [data_ref[pl.ds(2 * s + side + 16 * odd, 32, stride=32), :] for odd in range(2)]

    def join(even, odd):
        return jnp.where(left32, even, pltpu.roll(odd, HALF, 1))

    def join_right(even, odd):
        return jnp.where(left32, pltpu.roll(even, HALF, 1), odd)

    def v_rows(s):
        return jnp.concatenate(lines(s, 1), axis=0)[:, HALF:]

    def one_slice(s, carry):
        polar = lines(s, 0)
        for i, part in enumerate((*split(join(*polar)), *split(join_right(*polar)))):
            parts_ref[i] = part.astype(F32)
        slot = join(*lines(s, 1)).astype(jnp.int32)
        column = slot & 127
        moved = HALF + (column & 1) * 32 + ((column - HALF) >> 1)
        lines_ref[0] = (slot >> 7).astype(F32)
        lines_ref[1] = jnp.where(column < HALF, column, moved).astype(F32)

        def chunk(r):
            hit = repeated_row(lines_ref.at[0], r, 4) == row_iota
            first = [jnp.where(hit, repeated_row(parts_ref.at[i], r, 4), zero) for i in range(4)]
            place = repeated_row(lines_ref.at[1], r, 8) == column_iota
            return jnp.concatenate(first, axis=0), jnp.where(place, one, zero)

        dense = None
        for r in range(0, 32, 2):
            pairs = [chunk(r), chunk(r + 1)]
            first = jnp.concatenate([pair[0] for pair in pairs], axis=1)
            second = jnp.concatenate([pair[1] for pair in pairs], axis=1)
            term = lax.dot_general(
                first, second, (((1,), (1,)), ((), ())), preferred_element_type=F32
            )
            dense = term if dense is None else dense + term
        real = dense[0:64] + dense[64:128]
        imag = dense[128:192] + dense[192:256]
        dense_ref[s] = jnp.concatenate([real, imag], axis=1)
        return carry

    lax.fori_loop(0, 8, one_slice, 0)

    y = []
    for s in range(8):
        high, low = split(dense_ref[s])
        v_high, v_low = split(v_rows(s))
        y.append(dot(v_high, high) + dot(v_high, low) + dot(v_low, high))
    for s in range(8):
        source_real, source_imag = y[s][:, :HALF], y[s][:, LANES : LANES + HALF]
        if s == 0:
            real, imag = source_real, source_imag
        else:
            couple_real = SCREEN * y[s][:, HALF:LANES]
            couple_imag = SCREEN * y[s][:, LANES + HALF :]
            matrix = jnp.concatenate(
                [
                    jnp.concatenate([couple_real, -couple_imag], axis=1),
                    jnp.concatenate([couple_imag, couple_real], axis=1),
                ],
                axis=0,
            )
            m_high, m_low = split(matrix)
            x_high, x_low = split(jnp.concatenate([real, imag], axis=0))
            product = dot(m_high, x_high) + dot(m_high, x_low) + dot(m_low, x_high)
            real = product[:HALF] + source_real
            imag = product[HALF:] + source_imag
        out_ref[s, 0] = jnp.concatenate([real[:32], real[32:]], axis=1)
        out_ref[s, 1] = jnp.concatenate([imag[:32], imag[32:]], axis=1)


def tables(count):
    half = np.arange(count) + 0.5
    angle = np.outer(half, half) * (math.pi / count)
    table = np.concatenate([np.cos(angle), np.sin(angle)]).astype(np.float32)
    high = table.astype(jnp.bfloat16)
    low = (table - high.astype(np.float32)).astype(jnp.bfloat16)
    return np.concatenate([high, low])


def vmem(n):
    return [pl.BlockSpec(memory_space=pltpu.VMEM)] * n


def pack(lesser, greater):
    return pl.pallas_call(
        pack_kernel,
        out_shape=jax.ShapeDtypeStruct((64, 16, LANES), F32),
        in_specs=vmem(2),
        out_specs=vmem(1)[0],
        name="pack",
    )(lesser.reshape(512, LANES), greater.reshape(512, LANES))


def correlate(data, v_blocks, slots):
    return pl.pallas_call(
        correlate_kernel,
        out_shape=jax.ShapeDtypeStruct((1024, LANES), F32),
        in_specs=vmem(3) + [pl.BlockSpec(memory_space=pl.ANY)],
        out_specs=vmem(1)[0],
        scratch_shapes=[pltpu.VMEM((4, 512, 512), BF16), pltpu.SemaphoreType.DMA((4,))],
        compiler_params=pltpu.CompilerParams(vmem_limit_bytes=40 << 20),
        name="correlate",
    )(data.reshape(64, 2, 8, LANES), v_blocks, slots.reshape(32, LANES), jnp.asarray(tables(512)))


def screen(data):
    return pl.pallas_call(
        screen_kernel,
        out_shape=jax.ShapeDtypeStruct((8, 2, 32, LANES), F32),
        in_specs=vmem(1),
        out_specs=vmem(1)[0],
        scratch_shapes=[
            pltpu.VMEM((4, 32, LANES), F32),
            pltpu.VMEM((2, 32, LANES), F32),
            pltpu.VMEM((8, HALF, 256), F32),
        ],
        compiler_params=pltpu.CompilerParams(vmem_limit_bytes=40 << 20),
        name="screen",
    )(data)


def shards(g_lesser, g_greater, v_blocks, slots):
    data = lax.all_to_all(pack(g_lesser, g_greater), "energy", 0, 0, tiled=True)
    data = correlate(data, v_blocks, slots).reshape(512, 1, 256)
    data = lax.all_to_all(data, ("energy", "cuts"), 0, 0, tiled=True)
    blocks = screen(data.reshape(1024, LANES)).reshape(8, 64, LANES)
    blocks = lax.all_to_all(blocks, "cuts", 0, 0, tiled=True)
    return blocks.reshape(8, 2, 4096).transpose(1, 0, 2).reshape(2, 8, 1, 4096)


def solution(mesh):
    placed = (
        P(None, "energy", "cuts", None),
        P(None, "energy", "cuts", None),
        P("cuts", None, None),
        P("cuts", None),
    )
    return jax.shard_map(
        shards,
        mesh=mesh,
        in_specs=placed,
        out_specs=P(None, "energy", "cuts", None),
        check_vma=False,
    )
```

time: 112 us -> 98.3 us (0.88)
  the two profiles are of different devices: /device:TPU:2 before, /device:TPU:9 now
where the time goes in v2:
time: 98.3 us; the launch traced here: 97.9 us
  blocking collectives  81.6 us (83%)
  Pallas kernels  13.8 us (14%)
  local copies, waits for them, and re-layouts  2.59 us (3%)
    all_to_all x1, blocking collectives, shards(): data = lax.all_to_all(data, ('energy', 'cuts'), 0, 0, tiled=True)  38.6 us
    all_to_all x1, blocking collectives, shards(): data = lax.all_to_all(pack(g_lesser, g_greater), 'energy', 0, 0, tiled=True)  27.7 us
    all_to_all x1, blocking collectives, shards(): blocks = lax.all_to_all(blocks, 'cuts', 0, 0, tiled=True)  15.3 us
    pallas_call x1, Pallas kernels, screen(): pl.pallas_call(screen_kernel, out_shape=jax.ShapeDtypeStruct((8, 2, 32, L...  8.09 us
    pallas_call x1, Pallas kernels, correlate(): pl.pallas_call(correlate_kernel, out_shape=jax.ShapeDtypeStruct((1024, LA...  3.33 us
    pallas_call x1, Pallas kernels, pack(): pl.pallas_call(pack_kernel, out_shape=jax.ShapeDtypeStruct((64, 16, LANES...  2.35 us

profile of v2, /device:TPU:9, one launch (start us, length us, event | category | flops | bytes accessed | tf_op | source)
XLA Modules:
  0.0 97.9 jit_solution(3469673661938500810)
XLA Ops:
  0.0 0.0 copy-start
  0.0 2.4 %pack.1 = f32[64,16,128]{2,1,0:T(8,128)} custom-call(f32[512,128]{1,0:T(8,128)} %bitcast.16, f32[512,128]{1,0:T(8,128)} %bitcast.17), custom_call_target="tpu_custom_call" | custom-call | tf_op jit(solution)/shard_map/pack/pallas_call | solution.py:203
  2.4 27.7 %all_to_all.15 = f32[64,16,128]{2,1,0:T(8,128)S(1)} all-to-all(f32[64,16,128]{2,1,0:T(8,128)} %pack.1), channel_id=1, replica_groups=mesh['energy'=64,'cuts'=8] {'energy'}, dimensions={0} | all-to-all | bytes 1048576 | tf_op jit(solution)/shard_map/all_to_all | solution.py:241
  30.0 0.0 copy-done
  30.0 0.0 copy-start.1
  30.0 0.8 copy-done.1
  30.8 0.0 copy-start.2
  30.8 0.7 copy-done.2
  31.5 3.3 %correlate.1 = f32[1024,128]{1,0:T(8,128)S(1)} custom-call(f32[64,2,8,128]{3,2,1,0:T(8,128)S(1)} %bitcast.10, f32[1,64,64]{2,1,0:T(8,128)S(1)} %copy-done.1, s32[32,128]{1,0:T(8,128)S(1)} %bitcast.14, bf16[2048,512]{1,0:T(8,128)(2,1)S(1)} %copy-done), custom_call_target="tpu_custom_call" | custom-call | tf_op jit(solution)/shard_map/correlate/pallas_call | solution.py:213
  34.9 38.6 %all_to_all.16 = f32[512,1,256]{2,1,0:T(1,128)S(1)} all-to-all(f32[512,1,256]{2,1,0:T(1,128)S(1)} %bitcast.11), channel_id=1, replica_groups=mesh['energy'=64,'cuts'=8] {'energy','cuts'}, dimensions={0} | all-to-all | bytes 1048576 | tf_op jit(solution)/shard_map/all_to_all | solution.py:243
  73.5 8.1 %screen.1 = f32[8,2,32,128]{3,2,1,0:T(8,128)S(1)} custom-call(f32[1024,128]{1,0:T(8,128)S(1)} %bitcast.12), custom_call_target="tpu_custom_call" | custom-call | tf_op jit(solution)/shard_map/screen/pallas_call | solution.py:225
  81.6 15.3 %all_to_all.17 = f32[8,64,128]{2,1,0:T(8,128)S(1)} all-to-all(f32[8,64,128]{2,1,0:T(8,128)S(1)} %bitcast.13), channel_id=1, replica_groups=mesh['energy'=64,'cuts'=8] {'cuts'}, dimensions={0} | all-to-all | bytes 524288 | tf_op jit(solution)/shard_map/all_to_all | solution.py:245
  96.8 0.1 reshape.34
  97.0 1.0 copy.8
Async XLA Ops:
  0.0 30.0 %copy-start = (bf16[2048,512]{1,0:T(8,128)(2,1)S(1)}, bf16[2048,512]{1,0:T(8,128)(2,1)}, u32[]{:S(2)}) copy-start(bf16[2048,512]{1,0:T(8,128)(2,1)} %constant.2.clone.table_hbm) | copy-start | bytes 6291460
  30.0 0.8 copy-start.1
  30.8 0.7 copy-start.2

commit v3 on v2

--- a/solution.py
+++ b/solution.py
@@ -29,7 +29,16 @@
     return jnp.dot(a, b, preferred_element_type=F32)
 
 
-def pack_kernel(lesser_ref, greater_ref, out_ref):
+def pack_kernel(
+    lesser_ref, greater_ref, v_ref, slots_ref, table_hbm, out_ref, side_ref, table_ref, sem
+):
+    copy = pltpu.make_async_copy(table_hbm, table_ref, sem)
+    copy.start()
+    me = lax.axis_index("energy")
+    slot = slots_ref[pl.ds(me // 2, 1), :].astype(F32)
+    slot = jnp.where(me % 2 == 0, slot, pltpu.roll(slot, HALF, 1))[:, :HALF]
+    side = jnp.concatenate([slot, v_ref[0, pl.ds(me, 1), :]], axis=1)
+    side_ref[...] = jnp.broadcast_to(side, (8, LANES))
     left = left_half((8, LANES))
     for tile in range(32):
         for which, ref in enumerate((lesser_ref, greater_ref)):
@@ -38,38 +47,26 @@
             rows = pl.ds(which * 8, 8)
             out_ref[2 * tile, rows, :] = jnp.where(left, real, pltpu.roll(imag, HALF, 1))
             out_ref[2 * tile + 1, rows, :] = jnp.where(left, pltpu.roll(real, HALF, 1), imag)
-
-
-def correlate_kernel(data_ref, v_ref, slots_ref, table_hbm, out_ref, table_ref, sems):
+    copy.wait()
+
+
+def correlate_kernel(data_ref, side_ref, table_ref, out_ref):
     count = 512
-    copies = []
-    for i in range(4):
-        rows = pl.ds(i * count, count)
-        copies.append(pltpu.make_async_copy(table_hbm.at[rows], table_ref.at[i], sems.at[i]))
-        copies[i].start()
     left = left_half((count, LANES))
     sign = jnp.where(left, 1.0, -1.0).astype(F32)
 
     def turned(x):
         return pltpu.roll(x, HALF, 1)
 
-    me = lax.axis_index("energy")
-    slot = slots_ref[pl.ds(me // 2, 1), :].astype(F32)
-    slot = jnp.where(me % 2 == 0, slot, turned(slot))[:, :HALF]
-    side = jnp.concatenate([slot, v_ref[0, pl.ds(me, 1), :]], axis=1)
-    out_ref[pl.ds(1, count, stride=2), :] = jnp.broadcast_to(side, (count, LANES))
+    out_ref[pl.ds(1, count, stride=2), :] = jnp.broadcast_to(side_ref[pl.ds(0, 1), :], (count, LANES))
 
     lesser = data_ref[:, 0].reshape(count, LANES)
     greater = data_ref[:, 1].reshape(count, LANES)
     sig_high, sig_low = split(jnp.concatenate([lesser, greater], axis=1))
     both = jnp.concatenate([sig_high, sig_low], axis=1)
-    copies[0].wait()
     cosines = dot(table_ref[0], both)
-    copies[1].wait()
     sines = dot(table_ref[1], both)
-    copies[2].wait()
     cosines = cosines[:, :256] + cosines[:, 256:] + dot(table_ref[2], sig_high)
-    copies[3].wait()
     sines = sines[:, :256] + sines[:, 256:] + dot(table_ref[3], sig_high)
     cos_a, cos_b = cosines[:, :LANES], cosines[:, LANES:]
     sin_a, sin_b = sines[:, :LANES], sines[:, LANES:]
@@ -192,33 +189,43 @@
     table = np.concatenate([np.cos(angle), np.sin(angle)]).astype(np.float32)
     high = table.astype(jnp.bfloat16)
     low = (table - high.astype(np.float32)).astype(jnp.bfloat16)
-    return np.concatenate([high, low])
+    return np.concatenate([high, low]).reshape(4, count, count)
 
 
 def vmem(n):
     return [pl.BlockSpec(memory_space=pltpu.VMEM)] * n
 
 
-def pack(lesser, greater):
+def pack(lesser, greater, v_blocks, slots):
     return pl.pallas_call(
         pack_kernel,
-        out_shape=jax.ShapeDtypeStruct((64, 16, LANES), F32),
-        in_specs=vmem(2),
-        out_specs=vmem(1)[0],
+        out_shape=(
+            pltpu.VMEM((64, 16, LANES), F32),
+            pltpu.VMEM((8, LANES), F32),
+            pltpu.VMEM((4, 512, 512), BF16),
+        ),
+        in_specs=vmem(4) + [pl.BlockSpec(memory_space=pl.ANY)],
+        out_specs=tuple(vmem(3)),
+        scratch_shapes=[pltpu.SemaphoreType.DMA],
         name="pack",
-    )(lesser.reshape(512, LANES), greater.reshape(512, LANES))
-
-
-def correlate(data, v_blocks, slots):
+    )(
+        lesser.reshape(512, LANES),
+        greater.reshape(512, LANES),
+        v_blocks,
+        slots.reshape(32, LANES),
+        jnp.asarray(tables(512)),
+    )
+
+
+def correlate(data, side, table):
     return pl.pallas_call(
         correlate_kernel,
         out_shape=jax.ShapeDtypeStruct((1024, LANES), F32),
-        in_specs=vmem(3) + [pl.BlockSpec(memory_space=pl.ANY)],
+        in_specs=vmem(3),
         out_specs=vmem(1)[0],
-        scratch_shapes=[pltpu.VMEM((4, 512, 512), BF16), pltpu.SemaphoreType.DMA((4,))],
         compiler_params=pltpu.CompilerParams(vmem_limit_bytes=40 << 20),
         name="correlate",
-    )(data.reshape(64, 2, 8, LANES), v_blocks, slots.reshape(32, LANES), jnp.asarray(tables(512)))
+    )(data.reshape(64, 2, 8, LANES), side, table)
 
 
 def screen(data):
@@ -238,8 +245,9 @@
 
 
 def shards(g_lesser, g_greater, v_blocks, slots):
-    data = lax.all_to_all(pack(g_lesser, g_greater), "energy", 0, 0, tiled=True)
-    data = correlate(data, v_blocks, slots).reshape(512, 1, 256)
+    data, side, table = pack(g_lesser, g_greater, v_blocks, slots)
+    data = lax.all_to_all(data, "energy", 0, 0, tiled=True)
+    data = correlate(data, side, table).reshape(512, 1, 256)
     data = lax.all_to_all(data, ("energy", "cuts"), 0, 0, tiled=True)
     blocks = screen(data.reshape(1024, LANES)).reshape(8, 64, LANES)
     blocks = lax.all_to_all(blocks, "cuts", 0, 0, tiled=True)

time: 98.3 us -> 95.6 us (0.973)
  local copies, waits for them, and re-layouts: 2.59 us -> 1.11 us
    unnamed x6 -> x0, local copies, waits for them, and re-layouts: 1.48 us -> none
    pallas_call x1, Pallas kernels: 3.33 us -> 2.08 us  [correlate(): pl.pallas_call(correlate_kernel, out_shape=jax.ShapeDtypeStruct((1024, LA...]
where the time goes in v3:
time: 95.6 us; the launch traced here: 95.3 us
  blocking collectives  81.4 us (85%)
  Pallas kernels  12.9 us (13%)
  local copies, waits for them, and re-layouts  1.11 us (1%)
    all_to_all x1, blocking collectives, shards(): data = lax.all_to_all(data, ('energy', 'cuts'), 0, 0, tiled=True)  38.6 us
    all_to_all x1, blocking collectives, shards(): data = lax.all_to_all(data, 'energy', 0, 0, tiled=True)  27.5 us
    all_to_all x1, blocking collectives, shards(): blocks = lax.all_to_all(blocks, 'cuts', 0, 0, tiled=True)  15.3 us
    pallas_call x1, Pallas kernels, screen(): pl.pallas_call(screen_kernel, out_shape=jax.ShapeDtypeStruct((8, 2, 32, L...  8.09 us
    pallas_call x1, Pallas kernels, pack(): pl.pallas_call(pack_kernel, out_shape=(pltpu.VMEM((64, 16, LANES), F32),...  2.69 us
    pallas_call x1, Pallas kernels, correlate(): pl.pallas_call(correlate_kernel, out_shape=jax.ShapeDtypeStruct((1024, LA...  2.08 us

profile of v3, /device:TPU:9, one launch (start us, length us, event | category | flops | bytes accessed | tf_op | source)
XLA Modules:
  0.0 95.3 jit_solution(15998891708632302178)
XLA Ops:
  0.0 2.7 %pack.1 = (f32[64,16,128]{2,1,0:T(8,128)S(1)}, f32[8,128]{1,0:T(8,128)S(1)}, bf16[4,512,512]{2,1,0:T(8,128)(2,1)S(1)}) custom-call(f32[512,128]{1,0:T(8,128)} %bitcast.15, f32[512,128]{1,0:T(8,128)} %bitcast.16, f32[1,64,64]{2,1,0:T(8,128)} %v_ref.1, s32[32,128]{1,0:T(8,128)} %bitcast.17, bf16[4,512,512]{2,1,0:T(8,128)(2,1)} %constant.2.clone.table_hbm), custom_call_target="tpu_custom_call" | custom-call | tf_op jit(solution)/shard_map/pack/pallas_call | solution.py:200
  2.7 27.5 %all_to_all.15 = f32[64,16,128]{2,1,0:T(8,128)S(1)} all-to-all(f32[64,16,128]{2,1,0:T(8,128)S(1)} %get-tuple-element.8), channel_id=1, replica_groups=mesh['energy'=64,'cuts'=8] {'energy'}, dimensions={0} | all-to-all | bytes 1048576 | tf_op jit(solution)/shard_map/all_to_all | solution.py:249
  30.2 2.1 %correlate.1 = f32[1024,128]{1,0:T(8,128)S(1)} custom-call(f32[64,2,8,128]{3,2,1,0:T(8,128)S(1)} %bitcast.11, f32[8,128]{1,0:T(8,128)S(1)} %get-tuple-element.9.side_ref, bf16[4,512,512]{2,1,0:T(8,128)(2,1)S(1)} %get-tuple-element.10.table_ref), custom_call_target="tpu_custom_call" | custom-call | tf_op jit(solution)/shard_map/correlate/pallas_call | solution.py:221
  32.3 38.6 %all_to_all.16 = f32[512,1,256]{2,1,0:T(1,128)S(1)} all-to-all(f32[512,1,256]{2,1,0:T(1,128)S(1)} %bitcast.12), channel_id=1, replica_groups=mesh['energy'=64,'cuts'=8] {'energy','cuts'}, dimensions={0} | all-to-all | bytes 1048576 | tf_op jit(solution)/shard_map/all_to_all | solution.py:251
  70.9 8.1 %screen.1 = f32[8,2,32,128]{3,2,1,0:T(8,128)S(1)} custom-call(f32[1024,128]{1,0:T(8,128)S(1)} %bitcast.10), custom_call_target="tpu_custom_call" | custom-call | tf_op jit(solution)/shard_map/screen/pallas_call | solution.py:232
  79.0 15.3 %all_to_all.17 = f32[8,64,128]{2,1,0:T(8,128)S(1)} all-to-all(f32[8,64,128]{2,1,0:T(8,128)S(1)} %bitcast.13), channel_id=1, replica_groups=mesh['energy'=64,'cuts'=8] {'cuts'}, dimensions={0} | all-to-all | bytes 524288 | tf_op jit(solution)/shard_map/all_to_all | solution.py:253
  94.2 0.1 reshape.34
  94.4 1.0 %copy.8 = f32[2,8,1,4096]{3,2,1,0:T(1,128)} copy(f32[2,8,1,4096]{3,0,1,2:T(2,128)S(1)} %bitcast.14) | data formatting | bytes 524288 | tf_op jit(solution)/shard_map/reshape | solution.py:254

commit v4 on v3

--- a/solution.py
+++ b/solution.py
@@ -108,6 +108,7 @@
     left32 = left_half((32, LANES))
     row_iota = lax.broadcasted_iota(jnp.int32, (HALF, LANES), 0).astype(F32).astype(BF16)
     column_iota = lax.broadcasted_iota(jnp.int32, (LANES, LANES), 0).astype(F32).astype(BF16)
+    wide_iota = lax.broadcasted_iota(jnp.int32, (LANES, 256), 1).astype(F32).astype(BF16)
     zero = jnp.zeros((), BF16)
     one = jnp.ones((), BF16)
 
@@ -123,7 +124,7 @@
     def v_rows(s):
         return jnp.concatenate(lines(s, 1), axis=0)[:, HALF:]
 
-    def one_slice(s, carry):
+    def scatter(s, parts_ref, lines_ref):
         polar = lines(s, 0)
         for i, part in enumerate((*split(join(*polar)), *split(join_right(*polar)))):
             parts_ref[i] = part.astype(F32)
@@ -131,29 +132,49 @@
         column = slot & 127
         moved = HALF + (column & 1) * 32 + ((column - HALF) >> 1)
         lines_ref[0] = (slot >> 7).astype(F32)
-        lines_ref[1] = jnp.where(column < HALF, column, moved).astype(F32)
-
-        def chunk(r):
+        column = jnp.where(column < HALF, column, moved)
+        lines_ref[1] = column.astype(F32)
+        lines_ref[2] = ((slot >> 7) & 31).astype(F32)
+        places = (column + ((slot >> 12) << 7)).astype(F32).T.astype(BF16)
+
+        def tall(r):
             hit = repeated_row(lines_ref.at[0], r, 4) == row_iota
             first = [jnp.where(hit, repeated_row(parts_ref.at[i], r, 4), zero) for i in range(4)]
             place = repeated_row(lines_ref.at[1], r, 8) == column_iota
             return jnp.concatenate(first, axis=0), jnp.where(place, one, zero)
 
+        def wide(r):
+            hit = repeated_row(lines_ref.at[2], r, 2) == row_iota[:32]
+            first = [jnp.where(hit, repeated_row(parts_ref.at[i], r, 2), zero) for i in range(4)]
+            place = jnp.broadcast_to(places[:, r : r + 1], (LANES, 256)) == wide_iota
+            return jnp.concatenate(first, axis=0), jnp.where(place, one, zero)
+
         dense = None
+        other = None
         for r in range(0, 32, 2):
-            pairs = [chunk(r), chunk(r + 1)]
-            first = jnp.concatenate([pair[0] for pair in pairs], axis=1)
-            second = jnp.concatenate([pair[1] for pair in pairs], axis=1)
-            term = lax.dot_general(
-                first, second, (((1,), (1,)), ((), ())), preferred_element_type=F32
-            )
-            dense = term if dense is None else dense + term
+            if r % 4 == 2:
+                pairs = [wide(r), wide(r + 1)]
+                first = jnp.concatenate([pair[0] for pair in pairs], axis=1)
+                term = dot(first, jnp.concatenate([pair[1] for pair in pairs], axis=0))
+                other = term if other is None else other + term
+            else:
+                pairs = [tall(r), tall(r + 1)]
+                first = jnp.concatenate([pair[0] for pair in pairs], axis=1)
+                second = jnp.concatenate([pair[1] for pair in pairs], axis=1)
+                term = lax.dot_general(
+                    first, second, (((1,), (1,)), ((), ())), preferred_element_type=F32
+                )
+                dense = term if dense is None else dense + term
         real = dense[0:64] + dense[64:128]
         imag = dense[128:192] + dense[192:256]
+        other_real = other[0:32] + other[32:64]
+        other_imag = other[64:96] + other[96:128]
+        real += jnp.concatenate([other_real[:, :LANES], other_real[:, LANES:]], axis=0)
+        imag += jnp.concatenate([other_imag[:, :LANES], other_imag[:, LANES:]], axis=0)
         dense_ref[s] = jnp.concatenate([real, imag], axis=1)
-        return carry
-
-    lax.fori_loop(0, 8, one_slice, 0)
+
+    for s in range(8):
+        scatter(s, parts_ref.at[s], lines_ref.at[s])
 
     y = []
     for s in range(8):
@@ -235,8 +256,8 @@
         in_specs=vmem(1),
         out_specs=vmem(1)[0],
         scratch_shapes=[
-            pltpu.VMEM((4, 32, LANES), F32),
-            pltpu.VMEM((2, 32, LANES), F32),
+            pltpu.VMEM((8, 4, 32, LANES), F32),
+            pltpu.VMEM((8, 3, 32, LANES), F32),
             pltpu.VMEM((8, HALF, 256), F32),
         ],
         compiler_params=pltpu.CompilerParams(vmem_limit_bytes=40 << 20),

time: 95.6 us -> 93.2 us (0.975)
  Pallas kernels: 12.9 us -> 10.5 us
    pallas_call x1, Pallas kernels: 8.09 us -> 5.72 us  [screen(): pl.pallas_call(screen_kernel, out_shape=jax.ShapeDtypeStruct((8, 2, 32, L...]
where the time goes in v4:
time: 93.2 us; the launch traced here: 93 us
  blocking collectives  81.4 us (87%)
  Pallas kernels  10.5 us (11%)
  local copies, waits for them, and re-layouts  1.11 us (1%)
    all_to_all x1, blocking collectives, shards(): data = lax.all_to_all(data, ('energy', 'cuts'), 0, 0, tiled=True)  38.6 us
    all_to_all x1, blocking collectives, shards(): data = lax.all_to_all(data, 'energy', 0, 0, tiled=True)  27.5 us
    all_to_all x1, blocking collectives, shards(): blocks = lax.all_to_all(blocks, 'cuts', 0, 0, tiled=True)  15.3 us
    pallas_call x1, Pallas kernels, screen(): pl.pallas_call(screen_kernel, out_shape=jax.ShapeDtypeStruct((8, 2, 32, L...  5.72 us
    pallas_call x1, Pallas kernels, pack(): pl.pallas_call(pack_kernel, out_shape=(pltpu.VMEM((64, 16, LANES), F32),...  2.69 us
    pallas_call x1, Pallas kernels, correlate(): pl.pallas_call(correlate_kernel, out_shape=jax.ShapeDtypeStruct((1024, LA...  2.08 us

profile of v4, /device:TPU:9, one launch (start us, length us, event | category | flops | bytes accessed | tf_op | source)
XLA Modules:
  0.0 93.0 jit_solution(7930847947697668045)
XLA Ops:
  0.0 2.7 %pack.1 = (f32[64,16,128]{2,1,0:T(8,128)S(1)}, f32[8,128]{1,0:T(8,128)S(1)}, bf16[4,512,512]{2,1,0:T(8,128)(2,1)S(1)}) custom-call(f32[512,128]{1,0:T(8,128)} %bitcast.15, f32[512,128]{1,0:T(8,128)} %bitcast.16, f32[1,64,64]{2,1,0:T(8,128)} %v_ref.1, s32[32,128]{1,0:T(8,128)} %bitcast.17, bf16[4,512,512]{2,1,0:T(8,128)(2,1)} %constant.2.clone.table_hbm), custom_call_target="tpu_custom_call" | custom-call | tf_op jit(solution)/shard_map/pack/pallas_call | solution.py:221
  2.7 27.5 %all_to_all.15 = f32[64,16,128]{2,1,0:T(8,128)S(1)} all-to-all(f32[64,16,128]{2,1,0:T(8,128)S(1)} %get-tuple-element.8), channel_id=1, replica_groups=mesh['energy'=64,'cuts'=8] {'energy'}, dimensions={0} | all-to-all | bytes 1048576 | tf_op jit(solution)/shard_map/all_to_all | solution.py:270
  30.2 2.1 %correlate.1 = f32[1024,128]{1,0:T(8,128)S(1)} custom-call(f32[64,2,8,128]{3,2,1,0:T(8,128)S(1)} %bitcast.11, f32[8,128]{1,0:T(8,128)S(1)} %get-tuple-element.9.side_ref, bf16[4,512,512]{2,1,0:T(8,128)(2,1)S(1)} %get-tuple-element.10.table_ref), custom_call_target="tpu_custom_call" | custom-call | tf_op jit(solution)/shard_map/correlate/pallas_call | solution.py:242
  32.3 38.6 %all_to_all.16 = f32[512,1,256]{2,1,0:T(1,128)S(1)} all-to-all(f32[512,1,256]{2,1,0:T(1,128)S(1)} %bitcast.12), channel_id=1, replica_groups=mesh['energy'=64,'cuts'=8] {'energy','cuts'}, dimensions={0} | all-to-all | bytes 1048576 | tf_op jit(solution)/shard_map/all_to_all | solution.py:272
  70.9 5.7 %screen.1 = f32[8,2,32,128]{3,2,1,0:T(8,128)S(1)} custom-call(f32[1024,128]{1,0:T(8,128)S(1)} %bitcast.10), custom_call_target="tpu_custom_call" | custom-call | tf_op jit(solution)/shard_map/screen/pallas_call | solution.py:253
  76.6 15.3 %all_to_all.17 = f32[8,64,128]{2,1,0:T(8,128)S(1)} all-to-all(f32[8,64,128]{2,1,0:T(8,128)S(1)} %bitcast.13), channel_id=1, replica_groups=mesh['energy'=64,'cuts'=8] {'cuts'}, dimensions={0} | all-to-all | bytes 524288 | tf_op jit(solution)/shard_map/all_to_all | solution.py:274
  91.9 0.1 reshape.34
  92.0 1.0 %copy.8 = f32[2,8,1,4096]{3,2,1,0:T(1,128)} copy(f32[2,8,1,4096]{3,0,1,2:T(2,128)S(1)} %bitcast.14) | data formatting | bytes 524288 | tf_op jit(solution)/shard_map/reshape | solution.py:275

commit v5 on v4

--- a/solution.py
+++ b/solution.py
@@ -30,24 +30,35 @@
 
 
 def pack_kernel(
-    lesser_ref, greater_ref, v_ref, slots_ref, table_hbm, out_ref, side_ref, table_ref, sem
+    lesser_hbm, greater_hbm, table_hbm, v_hbm, slots_hbm, out_ref, side_ref, table_ref,
+    lesser_ref, greater_ref, v_ref, slots_ref, sems,
 ):
-    copy = pltpu.make_async_copy(table_hbm, table_ref, sem)
-    copy.start()
+    copies = [
+        pltpu.make_async_copy(lesser_hbm, lesser_ref, sems.at[0]),
+        pltpu.make_async_copy(greater_hbm, greater_ref, sems.at[1]),
+    ]
+    for i in range(4):
+        copies.append(pltpu.make_async_copy(table_hbm.at[i], table_ref.at[i], sems.at[2 + i]))
+    copies.append(pltpu.make_async_copy(v_hbm, v_ref, sems.at[6]))
+    copies.append(pltpu.make_async_copy(slots_hbm, slots_ref, sems.at[7]))
+    for copy in copies:
+        copy.start()
+    left = left_half((8, LANES))
+    for which, ref in enumerate((lesser_ref, greater_ref)):
+        copies[which].wait()
+        for tile in range(32):
+            real = ref[pl.ds(tile, 8, stride=32), :]
+            imag = ref[pl.ds(256 + tile, 8, stride=32), :]
+            rows = pl.ds(which * 8, 8)
+            out_ref[2 * tile, rows, :] = jnp.where(left, real, pltpu.roll(imag, HALF, 1))
+            out_ref[2 * tile + 1, rows, :] = jnp.where(left, pltpu.roll(real, HALF, 1), imag)
+    for copy in copies[2:]:
+        copy.wait()
     me = lax.axis_index("energy")
     slot = slots_ref[pl.ds(me // 2, 1), :].astype(F32)
     slot = jnp.where(me % 2 == 0, slot, pltpu.roll(slot, HALF, 1))[:, :HALF]
     side = jnp.concatenate([slot, v_ref[0, pl.ds(me, 1), :]], axis=1)
     side_ref[...] = jnp.broadcast_to(side, (8, LANES))
-    left = left_half((8, LANES))
-    for tile in range(32):
-        for which, ref in enumerate((lesser_ref, greater_ref)):
-            real = ref[pl.ds(tile, 8, stride=32), :]
-            imag = ref[pl.ds(256 + tile, 8, stride=32), :]
-            rows = pl.ds(which * 8, 8)
-            out_ref[2 * tile, rows, :] = jnp.where(left, real, pltpu.roll(imag, HALF, 1))
-            out_ref[2 * tile + 1, rows, :] = jnp.where(left, pltpu.roll(real, HALF, 1), imag)
-    copy.wait()
 
 
 def correlate_kernel(data_ref, side_ref, table_ref, out_ref):
@@ -181,27 +192,37 @@
         high, low = split(dense_ref[s])
         v_high, v_low = split(v_rows(s))
         y.append(dot(v_high, high) + dot(v_high, low) + dot(v_low, high))
+    def times(matrix, x):
+        m_high, m_low = split(matrix)
+        x_high, x_low = split(x)
+        return dot(m_high, x_high) + dot(m_high, x_low) + dot(m_low, x_high)
+
+    steps = []
     for s in range(8):
-        source_real, source_imag = y[s][:, :HALF], y[s][:, LANES : LANES + HALF]
-        if s == 0:
-            real, imag = source_real, source_imag
-        else:
-            couple_real = SCREEN * y[s][:, HALF:LANES]
-            couple_imag = SCREEN * y[s][:, LANES + HALF :]
-            matrix = jnp.concatenate(
-                [
-                    jnp.concatenate([couple_real, -couple_imag], axis=1),
-                    jnp.concatenate([couple_imag, couple_real], axis=1),
-                ],
-                axis=0,
-            )
-            m_high, m_low = split(matrix)
-            x_high, x_low = split(jnp.concatenate([real, imag], axis=0))
-            product = dot(m_high, x_high) + dot(m_high, x_low) + dot(m_low, x_high)
-            real = product[:HALF] + source_real
-            imag = product[HALF:] + source_imag
-        out_ref[s, 0] = jnp.concatenate([real[:32], real[32:]], axis=1)
-        out_ref[s, 1] = jnp.concatenate([imag[:32], imag[32:]], axis=1)
+        source = jnp.concatenate([y[s][:, :HALF], y[s][:, LANES : LANES + HALF]], axis=0)
+        couple_real = SCREEN * y[s][:, HALF:LANES]
+        couple_imag = SCREEN * y[s][:, LANES + HALF :]
+        matrix = jnp.concatenate(
+            [
+                jnp.concatenate([couple_real, -couple_imag], axis=1),
+                jnp.concatenate([couple_imag, couple_real], axis=1),
+            ],
+            axis=0,
+        )
+        steps.append((matrix, source))
+    x = [steps[0][1]]
+    pairs = []
+    for s in (1, 3, 5):
+        joined = times(steps[s + 1][0], jnp.concatenate(steps[s], axis=1))
+        pairs.append((joined[:, :LANES], joined[:, LANES:] + steps[s + 1][1]))
+    for i, s in enumerate((1, 3, 5)):
+        x.append(times(steps[s][0], x[s - 1]) + steps[s][1])
+        x.append(times(pairs[i][0], x[s - 1]) + pairs[i][1])
+    x.append(times(steps[7][0], x[6]) + steps[7][1])
+    for s in range(8):
+        for part in range(2):
+            rows = x[s][part * HALF : (part + 1) * HALF]
+            out_ref[s, part] = jnp.concatenate([rows[:32], rows[32:]], axis=1)
 
 
 def tables(count):
@@ -225,16 +246,22 @@
             pltpu.VMEM((8, LANES), F32),
             pltpu.VMEM((4, 512, 512), BF16),
         ),
-        in_specs=vmem(4) + [pl.BlockSpec(memory_space=pl.ANY)],
+        in_specs=[pl.BlockSpec(memory_space=pl.ANY)] * 5,
         out_specs=tuple(vmem(3)),
-        scratch_shapes=[pltpu.SemaphoreType.DMA],
+        scratch_shapes=[
+            pltpu.VMEM((512, LANES), F32),
+            pltpu.VMEM((512, LANES), F32),
+            pltpu.VMEM((1, HALF, HALF), F32),
+            pltpu.VMEM((32, LANES), jnp.int32),
+            pltpu.SemaphoreType.DMA((8,)),
+        ],
         name="pack",
     )(
         lesser.reshape(512, LANES),
         greater.reshape(512, LANES),
+        jnp.asarray(tables(512)),
         v_blocks,
         slots.reshape(32, LANES),
-        jnp.asarray(tables(512)),
     )
 
 

time: 93.2 us -> 92.1 us (0.988)
  Pallas kernels: 10.5 us -> 9.34 us
where the time goes in v5:
time: 92.1 us; the launch traced here: 91.9 us
  blocking collectives  81.4 us (88%)
  Pallas kernels  9.34 us (10%)
  local copies, waits for them, and re-layouts  1.11 us (1%)
    all_to_all x1, blocking collectives, shards(): data = lax.all_to_all(data, ('energy', 'cuts'), 0, 0, tiled=True)  38.6 us
    all_to_all x1, blocking collectives, shards(): data = lax.all_to_all(data, 'energy', 0, 0, tiled=True)  27.5 us
    all_to_all x1, blocking collectives, shards(): blocks = lax.all_to_all(blocks, 'cuts', 0, 0, tiled=True)  15.3 us
    pallas_call x1, Pallas kernels, screen(): pl.pallas_call(screen_kernel, out_shape=jax.ShapeDtypeStruct((8, 2, 32, L...  5.45 us
    pallas_call x1, Pallas kernels, correlate(): pl.pallas_call(correlate_kernel, out_shape=jax.ShapeDtypeStruct((1024, LA...  2.07 us

profile of v5, /device:TPU:9, one launch (start us, length us, event | category | flops | bytes accessed | tf_op | source)
XLA Modules:
  0.0 91.9 jit_solution(5282913138390716573)
XLA Ops:
  0.0 1.8 %pack.1 = (f32[64,16,128]{2,1,0:T(8,128)S(1)}, f32[8,128]{1,0:T(8,128)S(1)}, bf16[4,512,512]{2,1,0:T(8,128)(2,1)S(1)}) custom-call(f32[512,128]{1,0:T(8,128)} %bitcast.15, f32[512,128]{1,0:T(8,128)} %bitcast.16, bf16[4,512,512]{2,1,0:T(8,128)(2,1)} %constant.2.clone.table_hbm, f32[1,64,64]{2,1,0:T(8,128)} %v_hbm.1, s32[32,128]{1,0:T(8,128)} %bitcast.17), custom_call_target="tpu_custom_call" | custom-call | tf_op jit(solution)/shard_map/pack/pallas_call | solution.py:242
  1.8 27.5 %all_to_all.15 = f32[64,16,128]{2,1,0:T(8,128)S(1)} all-to-all(f32[64,16,128]{2,1,0:T(8,128)S(1)} %get-tuple-element.8), channel_id=1, replica_groups=mesh['energy'=64,'cuts'=8] {'energy'}, dimensions={0} | all-to-all | bytes 1048576 | tf_op jit(solution)/shard_map/all_to_all | solution.py:297
  29.3 2.1 %correlate.1 = f32[1024,128]{1,0:T(8,128)S(1)} custom-call(f32[64,2,8,128]{3,2,1,0:T(8,128)S(1)} %bitcast.11, f32[8,128]{1,0:T(8,128)S(1)} %get-tuple-element.9.side_ref, bf16[4,512,512]{2,1,0:T(8,128)(2,1)S(1)} %get-tuple-element.10.table_ref), custom_call_target="tpu_custom_call" | custom-call | tf_op jit(solution)/shard_map/correlate/pallas_call | solution.py:269
  31.4 38.6 %all_to_all.16 = f32[512,1,256]{2,1,0:T(1,128)S(1)} all-to-all(f32[512,1,256]{2,1,0:T(1,128)S(1)} %bitcast.12), channel_id=1, replica_groups=mesh['energy'=64,'cuts'=8] {'energy','cuts'}, dimensions={0} | all-to-all | bytes 1048576 | tf_op jit(solution)/shard_map/all_to_all | solution.py:299
  70.0 5.4 %screen.1 = f32[8,2,32,128]{3,2,1,0:T(8,128)S(1)} custom-call(f32[1024,128]{1,0:T(8,128)S(1)} %bitcast.10), custom_call_target="tpu_custom_call" | custom-call | tf_op jit(solution)/shard_map/screen/pallas_call | solution.py:280
  75.5 15.3 %all_to_all.17 = f32[8,64,128]{2,1,0:T(8,128)S(1)} all-to-all(f32[8,64,128]{2,1,0:T(8,128)S(1)} %bitcast.13), channel_id=1, replica_groups=mesh['energy'=64,'cuts'=8] {'cuts'}, dimensions={0} | all-to-all | bytes 524288 | tf_op jit(solution)/shard_map/all_to_all | solution.py:301
  90.7 0.1 reshape.34
  90.9 1.0 %copy.8 = f32[2,8,1,4096]{3,2,1,0:T(1,128)} copy(f32[2,8,1,4096]{3,0,1,2:T(2,128)S(1)} %bitcast.14) | data formatting | bytes 524288 | tf_op jit(solution)/shard_map/reshape | solution.py:302

commit v6 on v5

--- a/solution.py
+++ b/solution.py
@@ -294,7 +294,7 @@
 
 def shards(g_lesser, g_greater, v_blocks, slots):
     data, side, table = pack(g_lesser, g_greater, v_blocks, slots)
-    data = lax.all_to_all(data, "energy", 0, 0, tiled=True)
+    data = lax.all_to_all(data.reshape(64, 1, 2048), "energy", 0, 0, tiled=True)
     data = correlate(data, side, table).reshape(512, 1, 256)
     data = lax.all_to_all(data, ("energy", "cuts"), 0, 0, tiled=True)
     blocks = screen(data.reshape(1024, LANES)).reshape(8, 64, LANES)

time: 92.1 us -> 92.1 us (level)
  no operation moved by 1% of the time
where the time goes in v6:
time: 92.1 us; the launch traced here: 91.9 us
  blocking collectives  81.4 us (88%)
  Pallas kernels  9.34 us (10%)
  local copies, waits for them, and re-layouts  1.11 us (1%)
    all_to_all x1, blocking collectives, shards(): data = lax.all_to_all(data, ('energy', 'cuts'), 0, 0, tiled=True)  38.6 us
    all_to_all x1, blocking collectives, shards(): data = lax.all_to_all(data.reshape(64, 1, 2048), 'energy', 0, 0, tiled=True)  27.5 us
    all_to_all x1, blocking collectives, shards(): blocks = lax.all_to_all(blocks, 'cuts', 0, 0, tiled=True)  15.3 us
    pallas_call x1, Pallas kernels, screen(): pl.pallas_call(screen_kernel, out_shape=jax.ShapeDtypeStruct((8, 2, 32, L...  5.45 us
    pallas_call x1, Pallas kernels, correlate(): pl.pallas_call(correlate_kernel, out_shape=jax.ShapeDtypeStruct((1024, LA...  2.07 us

profile of v6, /device:TPU:9, one launch (start us, length us, event | category | flops | bytes accessed | tf_op | source)
XLA Modules:
  0.0 91.9 jit_solution(5282913138390716573)
XLA Ops:
  0.0 1.8 %pack.1 = (f32[64,16,128]{2,1,0:T(8,128)S(1)}, f32[8,128]{1,0:T(8,128)S(1)}, bf16[4,512,512]{2,1,0:T(8,128)(2,1)S(1)}) custom-call(f32[512,128]{1,0:T(8,128)} %bitcast.17, f32[512,128]{1,0:T(8,128)} %bitcast.18, bf16[4,512,512]{2,1,0:T(8,128)(2,1)} %constant.2.clone.table_hbm, f32[1,64,64]{2,1,0:T(8,128)} %v_hbm.1, s32[32,128]{1,0:T(8,128)} %bitcast.19), custom_call_target="tpu_custom_call" | custom-call | tf_op jit(solution)/shard_map/pack/pallas_call | solution.py:242
  1.8 27.5 %all_to_all.15 = f32[64,1,2048]{2,1,0:T(1,128)S(1)} all-to-all(f32[64,1,2048]{2,1,0:T(1,128)S(1)} %bitcast.15), channel_id=1, replica_groups=mesh['energy'=64,'cuts'=8] {'energy'}, dimensions={0} | all-to-all | bytes 1048576 | tf_op jit(solution)/shard_map/all_to_all | solution.py:297
  29.3 2.1 %correlate.1 = f32[1024,128]{1,0:T(8,128)S(1)} custom-call(f32[64,2,8,128]{3,2,1,0:T(8,128)S(1)} %bitcast.12, f32[8,128]{1,0:T(8,128)S(1)} %get-tuple-element.9.side_ref, bf16[4,512,512]{2,1,0:T(8,128)(2,1)S(1)} %get-tuple-element.10.table_ref), custom_call_target="tpu_custom_call" | custom-call | tf_op jit(solution)/shard_map/correlate/pallas_call | solution.py:269
  31.4 38.6 %all_to_all.16 = f32[512,1,256]{2,1,0:T(1,128)S(1)} all-to-all(f32[512,1,256]{2,1,0:T(1,128)S(1)} %bitcast.13), channel_id=1, replica_groups=mesh['energy'=64,'cuts'=8] {'energy','cuts'}, dimensions={0} | all-to-all | bytes 1048576 | tf_op jit(solution)/shard_map/all_to_all | solution.py:299
  70.0 5.4 %screen.1 = f32[8,2,32,128]{3,2,1,0:T(8,128)S(1)} custom-call(f32[1024,128]{1,0:T(8,128)S(1)} %bitcast.11), custom_call_target="tpu_custom_call" | custom-call | tf_op jit(solution)/shard_map/screen/pallas_call | solution.py:280
  75.5 15.3 %all_to_all.17 = f32[8,64,128]{2,1,0:T(8,128)S(1)} all-to-all(f32[8,64,128]{2,1,0:T(8,128)S(1)} %bitcast.14), channel_id=1, replica_groups=mesh['energy'=64,'cuts'=8] {'cuts'}, dimensions={0} | all-to-all | bytes 524288 | tf_op jit(solution)/shard_map/all_to_all | solution.py:301
  90.7 0.1 reshape.38
  90.9 1.0 %copy.9 = f32[2,8,1,4096]{3,2,1,0:T(1,128)} copy(f32[2,8,1,4096]{3,0,1,2:T(2,128)S(1)} %bitcast.16) | data formatting | bytes 524288 | tf_op jit(solution)/shard_map/reshape | solution.py:302

commit v7 on v6

--- a/solution.py
+++ b/solution.py
@@ -292,6 +292,33 @@
     )(data)
 
 
+def place_kernel(blocks_ref, out_hbm, sems):
+    copies = []
+    for part in range(2):
+        for i in range(2):
+            rows = pl.ds(4 * i, 4)
+            copies.append(
+                pltpu.make_async_copy(
+                    blocks_ref.at[rows, part], out_hbm.at[part, rows], sems.at[part, i]
+                )
+            )
+    for copy in copies:
+        copy.start()
+    for copy in copies:
+        copy.wait()
+
+
+def place(blocks):
+    return pl.pallas_call(
+        place_kernel,
+        out_shape=jax.ShapeDtypeStruct((2, 8, 32, LANES), F32),
+        in_specs=vmem(1),
+        out_specs=pl.BlockSpec(memory_space=pl.ANY),
+        scratch_shapes=[pltpu.SemaphoreType.DMA((2, 2))],
+        name="place",
+    )(pltpu.with_memory_space_constraint(blocks.reshape(8, 2, 32, LANES), pltpu.VMEM))
+
+
 def shards(g_lesser, g_greater, v_blocks, slots):
     data, side, table = pack(g_lesser, g_greater, v_blocks, slots)
     data = lax.all_to_all(data.reshape(64, 1, 2048), "energy", 0, 0, tiled=True)
@@ -299,7 +326,7 @@
     data = lax.all_to_all(data, ("energy", "cuts"), 0, 0, tiled=True)
     blocks = screen(data.reshape(1024, LANES)).reshape(8, 64, LANES)
     blocks = lax.all_to_all(blocks, "cuts", 0, 0, tiled=True)
-    return blocks.reshape(8, 2, 4096).transpose(1, 0, 2).reshape(2, 8, 1, 4096)
+    return place(blocks).reshape(2, 8, 1, 4096)
 
 
 def solution(mesh):

time: 92.1 us -> 91.7 us (level)
  local copies, waits for them, and re-layouts: 1.11 us -> 0 us
    reshape x2 -> x0, local copies, waits for them, and re-layouts: 1.11 us -> none  [shards(): return blocks.reshape(8, 2, 4096).transpose(1, 0, 2).reshape(2, 8, 1, 4096)]
where the time goes in v7:
time: 91.7 us; the launch traced here: 91.5 us
  blocking collectives  81.4 us (89%)
  Pallas kernels  10.1 us (11%)
    all_to_all x1, blocking collectives, shards(): data = lax.all_to_all(data, ('energy', 'cuts'), 0, 0, tiled=True)  38.6 us
    all_to_all x1, blocking collectives, shards(): data = lax.all_to_all(data.reshape(64, 1, 2048), 'energy', 0, 0, tiled=True)  27.5 us
    all_to_all x1, blocking collectives, shards(): blocks = lax.all_to_all(blocks, 'cuts', 0, 0, tiled=True)  15.3 us
    pallas_call x1, Pallas kernels, screen(): pl.pallas_call(screen_kernel, out_shape=jax.ShapeDtypeStruct((8, 2, 32, L...  5.45 us
    pallas_call x1, Pallas kernels, correlate(): pl.pallas_call(correlate_kernel, out_shape=jax.ShapeDtypeStruct((1024, LA...  2.07 us

profile of v7, /device:TPU:9, one launch (start us, length us, event | category | flops | bytes accessed | tf_op | source)
XLA Modules:
  0.0 91.5 jit_solution(9196948843956793141)
XLA Ops:
  0.0 1.8 %pack.1 = (f32[64,16,128]{2,1,0:T(8,128)S(1)}, f32[8,128]{1,0:T(8,128)S(1)}, bf16[4,512,512]{2,1,0:T(8,128)(2,1)S(1)}) custom-call(f32[512,128]{1,0:T(8,128)} %bitcast.16, f32[512,128]{1,0:T(8,128)} %bitcast.17, bf16[4,512,512]{2,1,0:T(8,128)(2,1)} %constant.2.clone.table_hbm, f32[1,64,64]{2,1,0:T(8,128)} %v_hbm.1, s32[32,128]{1,0:T(8,128)} %bitcast.18), custom_call_target="tpu_custom_call" | custom-call | tf_op jit(solution)/shard_map/pack/pallas_call | solution.py:242
  1.8 27.5 %all_to_all.15 = f32[64,1,2048]{2,1,0:T(1,128)S(1)} all-to-all(f32[64,1,2048]{2,1,0:T(1,128)S(1)} %bitcast.15), channel_id=1, replica_groups=mesh['energy'=64,'cuts'=8] {'energy'}, dimensions={0} | all-to-all | bytes 1048576 | tf_op jit(solution)/shard_map/all_to_all | solution.py:324
  29.3 2.1 %correlate.1 = f32[1024,128]{1,0:T(8,128)S(1)} custom-call(f32[64,2,8,128]{3,2,1,0:T(8,128)S(1)} %bitcast.11, f32[8,128]{1,0:T(8,128)S(1)} %get-tuple-element.9.side_ref, bf16[4,512,512]{2,1,0:T(8,128)(2,1)S(1)} %get-tuple-element.10.table_ref), custom_call_target="tpu_custom_call" | custom-call | tf_op jit(solution)/shard_map/correlate/pallas_call | solution.py:269
  31.4 38.6 %all_to_all.16 = f32[512,1,256]{2,1,0:T(1,128)S(1)} all-to-all(f32[512,1,256]{2,1,0:T(1,128)S(1)} %bitcast.12), channel_id=1, replica_groups=mesh['energy'=64,'cuts'=8] {'energy','cuts'}, dimensions={0} | all-to-all | bytes 1048576 | tf_op jit(solution)/shard_map/all_to_all | solution.py:326
  70.0 5.4 %screen.1 = f32[8,2,32,128]{3,2,1,0:T(8,128)S(1)} custom-call(f32[1024,128]{1,0:T(8,128)S(1)} %bitcast.10), custom_call_target="tpu_custom_call" | custom-call | tf_op jit(solution)/shard_map/screen/pallas_call | solution.py:280
  75.5 15.3 %all_to_all.17 = f32[8,64,128]{2,1,0:T(8,128)S(1)} all-to-all(f32[8,64,128]{2,1,0:T(8,128)S(1)} %bitcast.13), channel_id=1, replica_groups=mesh['energy'=64,'cuts'=8] {'cuts'}, dimensions={0} | all-to-all | bytes 524288 | tf_op jit(solution)/shard_map/all_to_all | solution.py:328
  90.7 0.7 place.1

commit v8 on v7

--- a/solution.py
+++ b/solution.py
@@ -163,7 +163,7 @@
         dense = None
         other = None
         for r in range(0, 32, 2):
-            if r % 4 == 2:
+            if r % 16 in (2, 6, 8, 10, 14):
                 pairs = [wide(r), wide(r + 1)]
                 first = jnp.concatenate([pair[0] for pair in pairs], axis=1)
                 term = dot(first, jnp.concatenate([pair[1] for pair in pairs], axis=0))

time: 91.7 us -> 91.3 us (level)
  no operation moved by 1% of the time
where the time goes in v8:
time: 91.3 us; the launch traced here: 91.1 us
  blocking collectives  81.4 us (89%)
  Pallas kernels  9.69 us (11%)
    all_to_all x1, blocking collectives, shards(): data = lax.all_to_all(data, ('energy', 'cuts'), 0, 0, tiled=True)  38.6 us
    all_to_all x1, blocking collectives, shards(): data = lax.all_to_all(data.reshape(64, 1, 2048), 'energy', 0, 0, tiled=True)  27.5 us
    all_to_all x1, blocking collectives, shards(): blocks = lax.all_to_all(blocks, 'cuts', 0, 0, tiled=True)  15.3 us
    pallas_call x1, Pallas kernels, screen(): pl.pallas_call(screen_kernel, out_shape=jax.ShapeDtypeStruct((8, 2, 32, L...  5.07 us
    pallas_call x1, Pallas kernels, correlate(): pl.pallas_call(correlate_kernel, out_shape=jax.ShapeDtypeStruct((1024, LA...  2.07 us

profile of v8, /device:TPU:9, one launch (start us, length us, event | category | flops | bytes accessed | tf_op | source)
XLA Modules:
  0.0 91.1 jit_solution(16022516356946054716)
XLA Ops:
  0.0 1.8 %pack.1 = (f32[64,16,128]{2,1,0:T(8,128)S(1)}, f32[8,128]{1,0:T(8,128)S(1)}, bf16[4,512,512]{2,1,0:T(8,128)(2,1)S(1)}) custom-call(f32[512,128]{1,0:T(8,128)} %bitcast.16, f32[512,128]{1,0:T(8,128)} %bitcast.17, bf16[4,512,512]{2,1,0:T(8,128)(2,1)} %constant.2.clone.table_hbm, f32[1,64,64]{2,1,0:T(8,128)} %v_hbm.1, s32[32,128]{1,0:T(8,128)} %bitcast.18), custom_call_target="tpu_custom_call" | custom-call | tf_op jit(solution)/shard_map/pack/pallas_call | solution.py:242
  1.8 27.5 %all_to_all.15 = f32[64,1,2048]{2,1,0:T(1,128)S(1)} all-to-all(f32[64,1,2048]{2,1,0:T(1,128)S(1)} %bitcast.15), channel_id=1, replica_groups=mesh['energy'=64,'cuts'=8] {'energy'}, dimensions={0} | all-to-all | bytes 1048576 | tf_op jit(solution)/shard_map/all_to_all | solution.py:324
  29.3 2.1 %correlate.1 = f32[1024,128]{1,0:T(8,128)S(1)} custom-call(f32[64,2,8,128]{3,2,1,0:T(8,128)S(1)} %bitcast.11, f32[8,128]{1,0:T(8,128)S(1)} %get-tuple-element.9.side_ref, bf16[4,512,512]{2,1,0:T(8,128)(2,1)S(1)} %get-tuple-element.10.table_ref), custom_call_target="tpu_custom_call" | custom-call | tf_op jit(solution)/shard_map/correlate/pallas_call | solution.py:269
  31.4 38.6 %all_to_all.16 = f32[512,1,256]{2,1,0:T(1,128)S(1)} all-to-all(f32[512,1,256]{2,1,0:T(1,128)S(1)} %bitcast.12), channel_id=1, replica_groups=mesh['energy'=64,'cuts'=8] {'energy','cuts'}, dimensions={0} | all-to-all | bytes 1048576 | tf_op jit(solution)/shard_map/all_to_all | solution.py:326
  70.0 5.1 %screen.1 = f32[8,2,32,128]{3,2,1,0:T(8,128)S(1)} custom-call(f32[1024,128]{1,0:T(8,128)S(1)} %bitcast.10), custom_call_target="tpu_custom_call" | custom-call | tf_op jit(solution)/shard_map/screen/pallas_call | solution.py:280
  75.1 15.3 %all_to_all.17 = f32[8,64,128]{2,1,0:T(8,128)S(1)} all-to-all(f32[8,64,128]{2,1,0:T(8,128)S(1)} %bitcast.13), channel_id=1, replica_groups=mesh['energy'=64,'cuts'=8] {'cuts'}, dimensions={0} | all-to-all | bytes 524288 | tf_op jit(solution)/shard_map/all_to_all | solution.py:328
  90.3 0.7 place.1
